TPU v7x, 128 devices: a whole 4x4x4 slice. The times are simulated.
128 devices in a mesh: section: 16 (over z, x), bond: 8 (over y, core).
Axes of the slice: x: 4, y: 4, z: 4, core: 2. Of those that a mesh axis runs over, the one named last changes fastest.
Arguments:
- site_tensor: float32 [16, 3072, 4, 3072], P('section', None, None, 'bond'), may hold values from -0.109375 to 0.109375
- boundary: float32 [128, 3072], replicated, may hold values from -6 to 6
- selected: int32 [16, 128], P('section'), may hold values from 0 to 3
Outputs:
- chosen_prob: float32 [16, 128], P('section')
- exit_rows: float32 [16, 128, 3072], P('section', None, 'bond')
All inputs are finite; a program needn't handle non-finite values.
Results may differ from a plain program's by a relative error of at most 0.0003.
Values sent between devices are 32-bit elements; how exact they have to be, the bound alone decides.
A program may use at most 128 MiB of HBM per device.

v0:
```python
import jax
import jax.numpy as jnp
from jax import lax
from jax.sharding import PartitionSpec as P

BATCH = 64


def from_behind(array, axis, by):
    count = lax.axis_size(axis)
    pairs = [(i, i + by) for i in range(count) if 0 <= i + by < count]
    return lax.ppermute(array, axis, pairs)


def finish(amplitudes, chosen, block_rows, outcomes, columns, width):
    shaped = amplitudes.reshape(block_rows, outcomes, columns)
    partial_weight = jnp.sum(shaped * shaped, axis=2)
    weight = lax.psum(partial_weight, "bond")
    outcome_ids = jnp.arange(outcomes, dtype=jnp.int32)
    onehot = (chosen[:, None] == outcome_ids[None, :]).astype(jnp.float32)
    chosen_weight = jnp.sum(onehot * weight, axis=1)
    prob_block = chosen_weight / jnp.sum(weight, axis=1)
    chosen_row = jnp.sum(onehot[:, :, None] * shaped, axis=1)
    next_block = chosen_row / jnp.sqrt(chosen_weight / width + 1e-06)[:, None]
    return (prob_block, next_block)


def on_device(site_tensor, boundary, selected):
    width = site_tensor.shape[1]
    outcomes = site_tensor.shape[2]
    columns = site_tensor.shape[3]
    site_matrix = site_tensor[0].reshape(width, outcomes * columns)
    sections = lax.axis_size("section")
    section_index = lax.axis_index("section")
    total_rows = boundary.shape[0]
    block_rows = BATCH
    micro_count = total_rows // block_rows
    picks = selected[0]
    start_rows = jnp.zeros((block_rows, width), jnp.float32)
    prob_init = jnp.zeros((total_rows,), jnp.float32)
    rows_init = jnp.zeros((total_rows, columns), jnp.float32)

    def advance(step_index, carry):
        incoming, prob_out, rows_out = carry
        micro = step_index - section_index
        valid = jnp.logical_and(micro >= 0, micro < micro_count)
        slot = jnp.clip(micro, 0, micro_count - 1)
        feed = jnp.clip(step_index, 0, micro_count - 1).astype(jnp.int32)
        fresh = lax.dynamic_slice_in_dim(boundary, feed * block_rows, block_rows, 0)
        chosen = lax.dynamic_slice_in_dim(picks, slot * block_rows, block_rows, 0)
        current = jnp.where(section_index == 0, fresh, incoming)
        amplitudes = jnp.dot(
            current,
            site_matrix,
            precision=lax.Precision.HIGHEST,
            preferred_element_type=jnp.float32,
        )
        prob_block, next_block = finish(amplitudes, chosen, block_rows, outcomes, columns, width)
        old_prob = lax.dynamic_slice_in_dim(prob_out, slot * block_rows, block_rows, 0)
        old_rows = lax.dynamic_slice_in_dim(rows_out, slot * block_rows, block_rows, 0)
        prob_out = lax.dynamic_update_slice_in_dim(
            prob_out, jnp.where(valid, prob_block, old_prob), slot * block_rows, 0
        )
        rows_out = lax.dynamic_update_slice_in_dim(
            rows_out, jnp.where(valid, next_block, old_rows), slot * block_rows, 0
        )
        whole_rows = lax.all_gather(next_block, "bond", axis=1, tiled=True)
        incoming = from_behind(whole_rows, "section", 1)
        return (incoming, prob_out, rows_out)

    final_carry = lax.fori_loop(
        0, micro_count + sections - 1, advance, (start_rows, prob_init, rows_init)
    )
    return (final_carry[1][None, :], final_carry[2][None, :, :])


def solution(mesh):
    in_specs = (P("section", None, None, "bond"), P(), P("section", None))
    out_specs = (P("section", None), P("section", None, "bond"))
    return jax.shard_map(
        on_device, mesh=mesh, in_specs=in_specs, out_specs=out_specs, check_vma=False
    )
```

profile of v0, /device:TPU:96, one launch (start us, length us, event | category | flops | bytes accessed | tf_op | source)
XLA Modules:
  0.0 1322.7 jit_solution(2115595274633260697)
XLA Ops:
  0.7 16.5 %copy.5 = f32[384,8,4,384]{3,1,2,0:T(8,128)} copy(f32[384,8,4,384]{3,2,1,0:T(4,128)} %bitcast.10) | data formatting | bytes 37748736
  17.3 1304.8 %while.18 = (s32[]{:T(128)}, f32[64,3072]{1,0:T(8,128)S(1)}, f32[128]{0:T(128)S(1)}, f32[128,384]{1,0:T(8,128)S(1)}, s32[]{:T(128)}, /*index=5*/s32[128]{0:T(128...) while((s32[]{:T(128)}, f32[64,3072]{1,0:T(8,128)S(1)}, ...), condition=%wide.region_6.7_spmd, body=%wide.region_0.6_spmd.sunk | while | flops 3624494848 | bytes 26552424 | solution.py:71
  17.5 14.6 %fusion.17 = f32[64,1536]{1,0:T(8,128)S(1)} fusion(f32[3072,1536]{1,0:T(8,128)} %get-tuple-element.314, f32[64,3072]{1,0:T(8,128)S(1)} %get-tuple-element.293, f32[128,3072]{1,0:T(8,128)S(1)} %get-tuple-element.313, s32[]{:T(128)S(6)} %select_n.103, pred[]{:T(512)} %get-tuple-element.312), kind=kOutput, calls=%fused_computation.clone.1 | convolution fusion | flops 3624075264 | bytes 20840452 | tf_op jit(solution)/shard_map/while/body/eval_jaxpr/dot_general | solution.py:52
  32.7 25.9 %psum.13 = f32[64,4]{1,0:T(8,128)S(1)} all-reduce(f32[64,4]{1,0:T(8,128)S(1)} %get-tuple-element.271), channel_id=1, replica_groups=mesh['section'=16,'bond'=8] {'bond'}, use_global_device_ids=true, to_apply=%region_3.3 | all-reduce | flops 256 | bytes 2048 | tf_op jit(solution)/shard_map/while/body/eval_jaxpr/psum | solution.py:18
  75.8 20.4 %collective-permute-done = f32[64,3072]{1,0:T(8,128)S(1)} collective-permute-done((f32[64,3072]{1,0:T(8,128)S(1)}, f32[64,3072]{1,0:T(8,128)S(1)}, u32[]{:S(2)}, u32[]{:S(2)}) %collective-permute-start) | collective-permute-done | bytes 786464 | tf_op jit(solution)/shard_map/while/body/eval_jaxpr/ppermute | solution.py:12
  96.4 14.6 %fusion.17 = f32[64,1536]{1,0:T(8,128)S(1)} fusion(f32[3072,1536]{1,0:T(8,128)} %get-tuple-element.314, f32[64,3072]{1,0:T(8,128)S(1)} %get-tuple-element.293, f32[128,3072]{1,0:T(8,128)S(1)} %get-tuple-element.313, s32[]{:T(128)S(6)} %select_n.103, pred[]{:T(512)} %get-tuple-element.312), kind=kOutput, calls=%fused_computation.clone.1 | convolution fusion | flops 3624075264 | bytes 20840452 | tf_op jit(solution)/shard_map/while/body/eval_jaxpr/dot_general | solution.py:52
  111.6 23.6 %psum.13 = f32[64,4]{1,0:T(8,128)S(1)} all-reduce(f32[64,4]{1,0:T(8,128)S(1)} %get-tuple-element.271), channel_id=1, replica_groups=mesh['section'=16,'bond'=8] {'bond'}, use_global_device_ids=true, to_apply=%region_3.3 | all-reduce | flops 256 | bytes 2048 | tf_op jit(solution)/shard_map/while/body/eval_jaxpr/psum | solution.py:18
  135.6 13.4 %all_gather.9 = f32[64,3072]{1,0:T(8,128)S(1)} all-gather(f32[64,384]{1,0:T(8,128)S(1)} %get-tuple-element.275), channel_id=1, replica_groups=mesh['section'=16,'bond'=8] {'bond'}, dimensions={1}, use_global_device_ids=true | all-gather | bytes 884736 | tf_op jit(solution)/shard_map/while/body/eval_jaxpr/all_gather | solution.py:67
  151.0 21.9 %collective-permute-done = f32[64,3072]{1,0:T(8,128)S(1)} collective-permute-done((f32[64,3072]{1,0:T(8,128)S(1)}, f32[64,3072]{1,0:T(8,128)S(1)}, u32[]{:S(2)}, u32[]{:S(2)}) %collective-permute-start) | collective-permute-done | bytes 786464 | tf_op jit(solution)/shard_map/while/body/eval_jaxpr/ppermute | solution.py:12
  173.0 14.6 %fusion.17 = f32[64,1536]{1,0:T(8,128)S(1)} fusion(f32[3072,1536]{1,0:T(8,128)} %get-tuple-element.314, f32[64,3072]{1,0:T(8,128)S(1)} %get-tuple-element.293, f32[128,3072]{1,0:T(8,128)S(1)} %get-tuple-element.313, s32[]{:T(128)S(6)} %select_n.103, pred[]{:T(512)} %get-tuple-element.312), kind=kOutput, calls=%fused_computation.clone.1 | convolution fusion | flops 3624075264 | bytes 20840452 | tf_op jit(solution)/shard_map/while/body/eval_jaxpr/dot_general | solution.py:52
  188.2 23.6 %psum.13 = f32[64,4]{1,0:T(8,128)S(1)} all-reduce(f32[64,4]{1,0:T(8,128)S(1)} %get-tuple-element.271), channel_id=1, replica_groups=mesh['section'=16,'bond'=8] {'bond'}, use_global_device_ids=true, to_apply=%region_3.3 | all-reduce | flops 256 | bytes 2048 | tf_op jit(solution)/shard_map/while/body/eval_jaxpr/psum | solution.py:18
  212.2 13.4 %all_gather.9 = f32[64,3072]{1,0:T(8,128)S(1)} all-gather(f32[64,384]{1,0:T(8,128)S(1)} %get-tuple-element.275), channel_id=1, replica_groups=mesh['section'=16,'bond'=8] {'bond'}, dimensions={1}, use_global_device_ids=true | all-gather | bytes 884736 | tf_op jit(solution)/shard_map/while/body/eval_jaxpr/all_gather | solution.py:67
  227.6 21.9 %collective-permute-done = f32[64,3072]{1,0:T(8,128)S(1)} collective-permute-done((f32[64,3072]{1,0:T(8,128)S(1)}, f32[64,3072]{1,0:T(8,128)S(1)}, u32[]{:S(2)}, u32[]{:S(2)}) %collective-permute-start) | collective-permute-done | bytes 786464 | tf_op jit(solution)/shard_map/while/body/eval_jaxpr/ppermute | solution.py:12
  249.6 14.6 %fusion.17 = f32[64,1536]{1,0:T(8,128)S(1)} fusion(f32[3072,1536]{1,0:T(8,128)} %get-tuple-element.314, f32[64,3072]{1,0:T(8,128)S(1)} %get-tuple-element.293, f32[128,3072]{1,0:T(8,128)S(1)} %get-tuple-element.313, s32[]{:T(128)S(6)} %select_n.103, pred[]{:T(512)} %get-tuple-element.312), kind=kOutput, calls=%fused_computation.clone.1 | convolution fusion | flops 3624075264 | bytes 20840452 | tf_op jit(solution)/shard_map/while/body/eval_jaxpr/dot_general | solution.py:52
  264.8 23.6 %psum.13 = f32[64,4]{1,0:T(8,128)S(1)} all-reduce(f32[64,4]{1,0:T(8,128)S(1)} %get-tuple-element.271), channel_id=1, replica_groups=mesh['section'=16,'bond'=8] {'bond'}, use_global_device_ids=true, to_apply=%region_3.3 | all-reduce | flops 256 | bytes 2048 | tf_op jit(solution)/shard_map/while/body/eval_jaxpr/psum | solution.py:18
  288.9 13.4 %all_gather.9 = f32[64,3072]{1,0:T(8,128)S(1)} all-gather(f32[64,384]{1,0:T(8,128)S(1)} %get-tuple-element.275), channel_id=1, replica_groups=mesh['section'=16,'bond'=8] {'bond'}, dimensions={1}, use_global_device_ids=true | all-gather | bytes 884736 | tf_op jit(solution)/shard_map/while/body/eval_jaxpr/all_gather | solution.py:67
  304.2 21.9 %collective-permute-done = f32[64,3072]{1,0:T(8,128)S(1)} collective-permute-done((f32[64,3072]{1,0:T(8,128)S(1)}, f32[64,3072]{1,0:T(8,128)S(1)}, u32[]{:S(2)}, u32[]{:S(2)}) %collective-permute-start) | collective-permute-done | bytes 786464 | tf_op jit(solution)/shard_map/while/body/eval_jaxpr/ppermute | solution.py:12
  326.2 14.6 %fusion.17 = f32[64,1536]{1,0:T(8,128)S(1)} fusion(f32[3072,1536]{1,0:T(8,128)} %get-tuple-element.314, f32[64,3072]{1,0:T(8,128)S(1)} %get-tuple-element.293, f32[128,3072]{1,0:T(8,128)S(1)} %get-tuple-element.313, s32[]{:T(128)S(6)} %select_n.103, pred[]{:T(512)} %get-tuple-element.312), kind=kOutput, calls=%fused_computation.clone.1 | convolution fusion | flops 3624075264 | bytes 20840452 | tf_op jit(solution)/shard_map/while/body/eval_jaxpr/dot_general | solution.py:52
  341.4 23.6 %psum.13 = f32[64,4]{1,0:T(8,128)S(1)} all-reduce(f32[64,4]{1,0:T(8,128)S(1)} %get-tuple-element.271), channel_id=1, replica_groups=mesh['section'=16,'bond'=8] {'bond'}, use_global_device_ids=true, to_apply=%region_3.3 | all-reduce | flops 256 | bytes 2048 | tf_op jit(solution)/shard_map/while/body/eval_jaxpr/psum | solution.py:18
  365.5 13.4 %all_gather.9 = f32[64,3072]{1,0:T(8,128)S(1)} all-gather(f32[64,384]{1,0:T(8,128)S(1)} %get-tuple-element.275), channel_id=1, replica_groups=mesh['section'=16,'bond'=8] {'bond'}, dimensions={1}, use_global_device_ids=true | all-gather | bytes 884736 | tf_op jit(solution)/shard_map/while/body/eval_jaxpr/all_gather | solution.py:67
  380.8 21.9 %collective-permute-done = f32[64,3072]{1,0:T(8,128)S(1)} collective-permute-done((f32[64,3072]{1,0:T(8,128)S(1)}, f32[64,3072]{1,0:T(8,128)S(1)}, u32[]{:S(2)}, u32[]{:S(2)}) %collective-permute-start) | collective-permute-done | bytes 786464 | tf_op jit(solution)/shard_map/while/body/eval_jaxpr/ppermute | solution.py:12
  402.8 14.6 %fusion.17 = f32[64,1536]{1,0:T(8,128)S(1)} fusion(f32[3072,1536]{1,0:T(8,128)} %get-tuple-element.314, f32[64,3072]{1,0:T(8,128)S(1)} %get-tuple-element.293, f32[128,3072]{1,0:T(8,128)S(1)} %get-tuple-element.313, s32[]{:T(128)S(6)} %select_n.103, pred[]{:T(512)} %get-tuple-element.312), kind=kOutput, calls=%fused_computation.clone.1 | convolution fusion | flops 3624075264 | bytes 20840452 | tf_op jit(solution)/shard_map/while/body/eval_jaxpr/dot_general | solution.py:52
  418.1 23.6 %psum.13 = f32[64,4]{1,0:T(8,128)S(1)} all-reduce(f32[64,4]{1,0:T(8,128)S(1)} %get-tuple-element.271), channel_id=1, replica_groups=mesh['section'=16,'bond'=8] {'bond'}, use_global_device_ids=true, to_apply=%region_3.3 | all-reduce | flops 256 | bytes 2048 | tf_op jit(solution)/shard_map/while/body/eval_jaxpr/psum | solution.py:18
  442.1 13.4 %all_gather.9 = f32[64,3072]{1,0:T(8,128)S(1)} all-gather(f32[64,384]{1,0:T(8,128)S(1)} %get-tuple-element.275), channel_id=1, replica_groups=mesh['section'=16,'bond'=8] {'bond'}, dimensions={1}, use_global_device_ids=true | all-gather | bytes 884736 | tf_op jit(solution)/shard_map/while/body/eval_jaxpr/all_gather | solution.py:67
  457.4 21.9 %collective-permute-done = f32[64,3072]{1,0:T(8,128)S(1)} collective-permute-done((f32[64,3072]{1,0:T(8,128)S(1)}, f32[64,3072]{1,0:T(8,128)S(1)}, u32[]{:S(2)}, u32[]{:S(2)}) %collective-permute-start) | collective-permute-done | bytes 786464 | tf_op jit(solution)/shard_map/while/body/eval_jaxpr/ppermute | solution.py:12
  479.4 14.6 %fusion.17 = f32[64,1536]{1,0:T(8,128)S(1)} fusion(f32[3072,1536]{1,0:T(8,128)} %get-tuple-element.314, f32[64,3072]{1,0:T(8,128)S(1)} %get-tuple-element.293, f32[128,3072]{1,0:T(8,128)S(1)} %get-tuple-element.313, s32[]{:T(128)S(6)} %select_n.103, pred[]{:T(512)} %get-tuple-element.312), kind=kOutput, calls=%fused_computation.clone.1 | convolution fusion | flops 3624075264 | bytes 20840452 | tf_op jit(solution)/shard_map/while/body/eval_jaxpr/dot_general | solution.py:52
  494.7 23.6 %psum.13 = f32[64,4]{1,0:T(8,128)S(1)} all-reduce(f32[64,4]{1,0:T(8,128)S(1)} %get-tuple-element.271), channel_id=1, replica_groups=mesh['section'=16,'bond'=8] {'bond'}, use_global_device_ids=true, to_apply=%region_3.3 | all-reduce | flops 256 | bytes 2048 | tf_op jit(solution)/shard_map/while/body/eval_jaxpr/psum | solution.py:18
  534.0 21.9 %collective-permute-done = f32[64,3072]{1,0:T(8,128)S(1)} collective-permute-done((f32[64,3072]{1,0:T(8,128)S(1)}, f32[64,3072]{1,0:T(8,128)S(1)}, u32[]{:S(2)}, u32[]{:S(2)}) %collective-permute-start) | collective-permute-done | bytes 786464 | tf_op jit(solution)/shard_map/while/body/eval_jaxpr/ppermute | solution.py:12
  556.0 14.6 %fusion.17 = f32[64,1536]{1,0:T(8,128)S(1)} fusion(f32[3072,1536]{1,0:T(8,128)} %get-tuple-element.314, f32[64,3072]{1,0:T(8,128)S(1)} %get-tuple-element.293, f32[128,3072]{1,0:T(8,128)S(1)} %get-tuple-element.313, s32[]{:T(128)S(6)} %select_n.103, pred[]{:T(512)} %get-tuple-element.312), kind=kOutput, calls=%fused_computation.clone.1 | convolution fusion | flops 3624075264 | bytes 20840452 | tf_op jit(solution)/shard_map/while/body/eval_jaxpr/dot_general | solution.py:52
  571.3 23.6 %psum.13 = f32[64,4]{1,0:T(8,128)S(1)} all-reduce(f32[64,4]{1,0:T(8,128)S(1)} %get-tuple-element.271), channel_id=1, replica_groups=mesh['section'=16,'bond'=8] {'bond'}, use_global_device_ids=true, to_apply=%region_3.3 | all-reduce | flops 256 | bytes 2048 | tf_op jit(solution)/shard_map/while/body/eval_jaxpr/psum | solution.py:18
  595.3 13.4 %all_gather.9 = f32[64,3072]{1,0:T(8,128)S(1)} all-gather(f32[64,384]{1,0:T(8,128)S(1)} %get-tuple-element.275), channel_id=1, replica_groups=mesh['section'=16,'bond'=8] {'bond'}, dimensions={1}, use_global_device_ids=true | all-gather | bytes 884736 | tf_op jit(solution)/shard_map/while/body/eval_jaxpr/all_gather | solution.py:67
  610.6 21.9 %collective-permute-done = f32[64,3072]{1,0:T(8,128)S(1)} collective-permute-done((f32[64,3072]{1,0:T(8,128)S(1)}, f32[64,3072]{1,0:T(8,128)S(1)}, u32[]{:S(2)}, u32[]{:S(2)}) %collective-permute-start) | collective-permute-done | bytes 786464 | tf_op jit(solution)/shard_map/while/body/eval_jaxpr/ppermute | solution.py:12
  632.7 14.6 %fusion.17 = f32[64,1536]{1,0:T(8,128)S(1)} fusion(f32[3072,1536]{1,0:T(8,128)} %get-tuple-element.314, f32[64,3072]{1,0:T(8,128)S(1)} %get-tuple-element.293, f32[128,3072]{1,0:T(8,128)S(1)} %get-tuple-element.313, s32[]{:T(128)S(6)} %select_n.103, pred[]{:T(512)} %get-tuple-element.312), kind=kOutput, calls=%fused_computation.clone.1 | convolution fusion | flops 3624075264 | bytes 20840452 | tf_op jit(solution)/shard_map/while/body/eval_jaxpr/dot_general | solution.py:52
  647.9 23.6 %psum.13 = f32[64,4]{1,0:T(8,128)S(1)} all-reduce(f32[64,4]{1,0:T(8,128)S(1)} %get-tuple-element.271), channel_id=1, replica_groups=mesh['section'=16,'bond'=8] {'bond'}, use_global_device_ids=true, to_apply=%region_3.3 | all-reduce | flops 256 | bytes 2048 | tf_op jit(solution)/shard_map/while/body/eval_jaxpr/psum | solution.py:18
  671.9 13.4 %all_gather.9 = f32[64,3072]{1,0:T(8,128)S(1)} all-gather(f32[64,384]{1,0:T(8,128)S(1)} %get-tuple-element.275), channel_id=1, replica_groups=mesh['section'=16,'bond'=8] {'bond'}, dimensions={1}, use_global_device_ids=true | all-gather | bytes 884736 | tf_op jit(solution)/shard_map/while/body/eval_jaxpr/all_gather | solution.py:67
  687.3 21.9 %collective-permute-done = f32[64,3072]{1,0:T(8,128)S(1)} collective-permute-done((f32[64,3072]{1,0:T(8,128)S(1)}, f32[64,3072]{1,0:T(8,128)S(1)}, u32[]{:S(2)}, u32[]{:S(2)}) %collective-permute-start) | collective-permute-done | bytes 786464 | tf_op jit(solution)/shard_map/while/body/eval_jaxpr/ppermute | solution.py:12
  709.3 14.6 %fusion.17 = f32[64,1536]{1,0:T(8,128)S(1)} fusion(f32[3072,1536]{1,0:T(8,128)} %get-tuple-element.314, f32[64,3072]{1,0:T(8,128)S(1)} %get-tuple-element.293, f32[128,3072]{1,0:T(8,128)S(1)} %get-tuple-element.313, s32[]{:T(128)S(6)} %select_n.103, pred[]{:T(512)} %get-tuple-element.312), kind=kOutput, calls=%fused_computation.clone.1 | convolution fusion | flops 3624075264 | bytes 20840452 | tf_op jit(solution)/shard_map/while/body/eval_jaxpr/dot_general | solution.py:52
  724.5 23.6 %psum.13 = f32[64,4]{1,0:T(8,128)S(1)} all-reduce(f32[64,4]{1,0:T(8,128)S(1)} %get-tuple-element.271), channel_id=1, replica_groups=mesh['section'=16,'bond'=8] {'bond'}, use_global_device_ids=true, to_apply=%region_3.3 | all-reduce | flops 256 | bytes 2048 | tf_op jit(solution)/shard_map/while/body/eval_jaxpr/psum | solution.py:18
  748.6 13.4 %all_gather.9 = f32[64,3072]{1,0:T(8,128)S(1)} all-gather(f32[64,384]{1,0:T(8,128)S(1)} %get-tuple-element.275), channel_id=1, replica_groups=mesh['section'=16,'bond'=8] {'bond'}, dimensions={1}, use_global_device_ids=true | all-gather | bytes 884736 | tf_op jit(solution)/shard_map/while/body/eval_jaxpr/all_gather | solution.py:67
  763.9 21.9 %collective-permute-done = f32[64,3072]{1,0:T(8,128)S(1)} collective-permute-done((f32[64,3072]{1,0:T(8,128)S(1)}, f32[64,3072]{1,0:T(8,128)S(1)}, u32[]{:S(2)}, u32[]{:S(2)}) %collective-permute-start) | collective-permute-done | bytes 786464 | tf_op jit(solution)/shard_map/while/body/eval_jaxpr/ppermute | solution.py:12
  785.9 14.6 %fusion.17 = f32[64,1536]{1,0:T(8,128)S(1)} fusion(f32[3072,1536]{1,0:T(8,128)} %get-tuple-element.314, f32[64,3072]{1,0:T(8,128)S(1)} %get-tuple-element.293, f32[128,3072]{1,0:T(8,128)S(1)} %get-tuple-element.313, s32[]{:T(128)S(6)} %select_n.103, pred[]{:T(512)} %get-tuple-element.312), kind=kOutput, calls=%fused_computation.clone.1 | convolution fusion | flops 3624075264 | bytes 20840452 | tf_op jit(solution)/shard_map/while/body/eval_jaxpr/dot_general | solution.py:52
  801.1 23.6 %psum.13 = f32[64,4]{1,0:T(8,128)S(1)} all-reduce(f32[64,4]{1,0:T(8,128)S(1)} %get-tuple-element.271), channel_id=1, replica_groups=mesh['section'=16,'bond'=8] {'bond'}, use_global_device_ids=true, to_apply=%region_3.3 | all-reduce | flops 256 | bytes 2048 | tf_op jit(solution)/shard_map/while/body/eval_jaxpr/psum | solution.py:18
  825.2 13.4 %all_gather.9 = f32[64,3072]{1,0:T(8,128)S(1)} all-gather(f32[64,384]{1,0:T(8,128)S(1)} %get-tuple-element.275), channel_id=1, replica_groups=mesh['section'=16,'bond'=8] {'bond'}, dimensions={1}, use_global_device_ids=true | all-gather | bytes 884736 | tf_op jit(solution)/shard_map/while/body/eval_jaxpr/all_gather | solution.py:67
  840.5 21.9 %collective-permute-done = f32[64,3072]{1,0:T(8,128)S(1)} collective-permute-done((f32[64,3072]{1,0:T(8,128)S(1)}, f32[64,3072]{1,0:T(8,128)S(1)}, u32[]{:S(2)}, u32[]{:S(2)}) %collective-permute-start) | collective-permute-done | bytes 786464 | tf_op jit(solution)/shard_map/while/body/eval_jaxpr/ppermute | solution.py:12
  862.5 14.6 %fusion.17 = f32[64,1536]{1,0:T(8,128)S(1)} fusion(f32[3072,1536]{1,0:T(8,128)} %get-tuple-element.314, f32[64,3072]{1,0:T(8,128)S(1)} %get-tuple-element.293, f32[128,3072]{1,0:T(8,128)S(1)} %get-tuple-element.313, s32[]{:T(128)S(6)} %select_n.103, pred[]{:T(512)} %get-tuple-element.312), kind=kOutput, calls=%fused_computation.clone.1 | convolution fusion | flops 3624075264 | bytes 20840452 | tf_op jit(solution)/shard_map/while/body/eval_jaxpr/dot_general | solution.py:52
  877.7 23.6 %psum.13 = f32[64,4]{1,0:T(8,128)S(1)} all-reduce(f32[64,4]{1,0:T(8,128)S(1)} %get-tuple-element.271), channel_id=1, replica_groups=mesh['section'=16,'bond'=8] {'bond'}, use_global_device_ids=true, to_apply=%region_3.3 | all-reduce | flops 256 | bytes 2048 | tf_op jit(solution)/shard_map/while/body/eval_jaxpr/psum | solution.py:18
  901.8 13.4 %all_gather.9 = f32[64,3072]{1,0:T(8,128)S(1)} all-gather(f32[64,384]{1,0:T(8,128)S(1)} %get-tuple-element.275), channel_id=1, replica_groups=mesh['section'=16,'bond'=8] {'bond'}, dimensions={1}, use_global_device_ids=true | all-gather | bytes 884736 | tf_op jit(solution)/shard_map/while/body/eval_jaxpr/all_gather | solution.py:67
  917.1 21.9 %collective-permute-done = f32[64,3072]{1,0:T(8,128)S(1)} collective-permute-done((f32[64,3072]{1,0:T(8,128)S(1)}, f32[64,3072]{1,0:T(8,128)S(1)}, u32[]{:S(2)}, u32[]{:S(2)}) %collective-permute-start) | collective-permute-done | bytes 786464 | tf_op jit(solution)/shard_map/while/body/eval_jaxpr/ppermute | solution.py:12
  939.1 14.6 %fusion.17 = f32[64,1536]{1,0:T(8,128)S(1)} fusion(f32[3072,1536]{1,0:T(8,128)} %get-tuple-element.314, f32[64,3072]{1,0:T(8,128)S(1)} %get-tuple-element.293, f32[128,3072]{1,0:T(8,128)S(1)} %get-tuple-element.313, s32[]{:T(128)S(6)} %select_n.103, pred[]{:T(512)} %get-tuple-element.312), kind=kOutput, calls=%fused_computation.clone.1 | convolution fusion | flops 3624075264 | bytes 20840452 | tf_op jit(solution)/shard_map/while/body/eval_jaxpr/dot_general | solution.py:52
  954.4 23.6 %psum.13 = f32[64,4]{1,0:T(8,128)S(1)} all-reduce(f32[64,4]{1,0:T(8,128)S(1)} %get-tuple-element.271), channel_id=1, replica_groups=mesh['section'=16,'bond'=8] {'bond'}, use_global_device_ids=true, to_apply=%region_3.3 | all-reduce | flops 256 | bytes 2048 | tf_op jit(solution)/shard_map/while/body/eval_jaxpr/psum | solution.py:18
  978.4 13.4 %all_gather.9 = f32[64,3072]{1,0:T(8,128)S(1)} all-gather(f32[64,384]{1,0:T(8,128)S(1)} %get-tuple-element.275), channel_id=1, replica_groups=mesh['section'=16,'bond'=8] {'bond'}, dimensions={1}, use_global_device_ids=true | all-gather | bytes 884736 | tf_op jit(solution)/shard_map/while/body/eval_jaxpr/all_gather | solution.py:67
  993.7 21.9 %collective-permute-done = f32[64,3072]{1,0:T(8,128)S(1)} collective-permute-done((f32[64,3072]{1,0:T(8,128)S(1)}, f32[64,3072]{1,0:T(8,128)S(1)}, u32[]{:S(2)}, u32[]{:S(2)}) %collective-permute-start) | collective-permute-done | bytes 786464 | tf_op jit(solution)/shard_map/while/body/eval_jaxpr/ppermute | solution.py:12
  1015.7 14.6 %fusion.17 = f32[64,1536]{1,0:T(8,128)S(1)} fusion(f32[3072,1536]{1,0:T(8,128)} %get-tuple-element.314, f32[64,3072]{1,0:T(8,128)S(1)} %get-tuple-element.293, f32[128,3072]{1,0:T(8,128)S(1)} %get-tuple-element.313, s32[]{:T(128)S(6)} %select_n.103, pred[]{:T(512)} %get-tuple-element.312), kind=kOutput, calls=%fused_computation.clone.1 | convolution fusion | flops 3624075264 | bytes 20840452 | tf_op jit(solution)/shard_map/while/body/eval_jaxpr/dot_general | solution.py:52
  1031.0 23.6 %psum.13 = f32[64,4]{1,0:T(8,128)S(1)} all-reduce(f32[64,4]{1,0:T(8,128)S(1)} %get-tuple-element.271), channel_id=1, replica_groups=mesh['section'=16,'bond'=8] {'bond'}, use_global_device_ids=true, to_apply=%region_3.3 | all-reduce | flops 256 | bytes 2048 | tf_op jit(solution)/shard_map/while/body/eval_jaxpr/psum | solution.py:18
  1070.3 21.9 %collective-permute-done = f32[64,3072]{1,0:T(8,128)S(1)} collective-permute-done((f32[64,3072]{1,0:T(8,128)S(1)}, f32[64,3072]{1,0:T(8,128)S(1)}, u32[]{:S(2)}, u32[]{:S(2)}) %collective-permute-start) | collective-permute-done | bytes 786464 | tf_op jit(solution)/shard_map/while/body/eval_jaxpr/ppermute | solution.py:12
  1092.3 14.6 %fusion.17 = f32[64,1536]{1,0:T(8,128)S(1)} fusion(f32[3072,1536]{1,0:T(8,128)} %get-tuple-element.314, f32[64,3072]{1,0:T(8,128)S(1)} %get-tuple-element.293, f32[128,3072]{1,0:T(8,128)S(1)} %get-tuple-element.313, s32[]{:T(128)S(6)} %select_n.103, pred[]{:T(512)} %get-tuple-element.312), kind=kOutput, calls=%fused_computation.clone.1 | convolution fusion | flops 3624075264 | bytes 20840452 | tf_op jit(solution)/shard_map/while/body/eval_jaxpr/dot_general | solution.py:52
  1107.6 23.6 %psum.13 = f32[64,4]{1,0:T(8,128)S(1)} all-reduce(f32[64,4]{1,0:T(8,128)S(1)} %get-tuple-element.271), channel_id=1, replica_groups=mesh['section'=16,'bond'=8] {'bond'}, use_global_device_ids=true, to_apply=%region_3.3 | all-reduce | flops 256 | bytes 2048 | tf_op jit(solution)/shard_map/while/body/eval_jaxpr/psum | solution.py:18
  1146.9 21.9 %collective-permute-done = f32[64,3072]{1,0:T(8,128)S(1)} collective-permute-done((f32[64,3072]{1,0:T(8,128)S(1)}, f32[64,3072]{1,0:T(8,128)S(1)}, u32[]{:S(2)}, u32[]{:S(2)}) %collective-permute-start) | collective-permute-done | bytes 786464 | tf_op jit(solution)/shard_map/while/body/eval_jaxpr/ppermute | solution.py:12
  1169.0 14.6 %fusion.17 = f32[64,1536]{1,0:T(8,128)S(1)} fusion(f32[3072,1536]{1,0:T(8,128)} %get-tuple-element.314, f32[64,3072]{1,0:T(8,128)S(1)} %get-tuple-element.293, f32[128,3072]{1,0:T(8,128)S(1)} %get-tuple-element.313, s32[]{:T(128)S(6)} %select_n.103, pred[]{:T(512)} %get-tuple-element.312), kind=kOutput, calls=%fused_computation.clone.1 | convolution fusion | flops 3624075264 | bytes 20840452 | tf_op jit(solution)/shard_map/while/body/eval_jaxpr/dot_general | solution.py:52
  1184.2 23.6 %psum.13 = f32[64,4]{1,0:T(8,128)S(1)} all-reduce(f32[64,4]{1,0:T(8,128)S(1)} %get-tuple-element.271), channel_id=1, replica_groups=mesh['section'=16,'bond'=8] {'bond'}, use_global_device_ids=true, to_apply=%region_3.3 | all-reduce | flops 256 | bytes 2048 | tf_op jit(solution)/shard_map/while/body/eval_jaxpr/psum | solution.py:18
  1223.6 21.9 %collective-permute-done = f32[64,3072]{1,0:T(8,128)S(1)} collective-permute-done((f32[64,3072]{1,0:T(8,128)S(1)}, f32[64,3072]{1,0:T(8,128)S(1)}, u32[]{:S(2)}, u32[]{:S(2)}) %collective-permute-start) | collective-permute-done | bytes 786464 | tf_op jit(solution)/shard_map/while/body/eval_jaxpr/ppermute | solution.py:12
  1245.6 14.6 %fusion.17 = f32[64,1536]{1,0:T(8,128)S(1)} fusion(f32[3072,1536]{1,0:T(8,128)} %get-tuple-element.314, f32[64,3072]{1,0:T(8,128)S(1)} %get-tuple-element.293, f32[128,3072]{1,0:T(8,128)S(1)} %get-tuple-element.313, s32[]{:T(128)S(6)} %select_n.103, pred[]{:T(512)} %get-tuple-element.312), kind=kOutput, calls=%fused_computation.clone.1 | convolution fusion | flops 3624075264 | bytes 20840452 | tf_op jit(solution)/shard_map/while/body/eval_jaxpr/dot_general | solution.py:52
  1260.8 23.6 %psum.13 = f32[64,4]{1,0:T(8,128)S(1)} all-reduce(f32[64,4]{1,0:T(8,128)S(1)} %get-tuple-element.271), channel_id=1, replica_groups=mesh['section'=16,'bond'=8] {'bond'}, use_global_device_ids=true, to_apply=%region_3.3 | all-reduce | flops 256 | bytes 2048 | tf_op jit(solution)/shard_map/while/body/eval_jaxpr/psum | solution.py:18
  1300.2 21.9 %collective-permute-done = f32[64,3072]{1,0:T(8,128)S(1)} collective-permute-done((f32[64,3072]{1,0:T(8,128)S(1)}, f32[64,3072]{1,0:T(8,128)S(1)}, u32[]{:S(2)}, u32[]{:S(2)}) %collective-permute-start) | collective-permute-done | bytes 786464 | tf_op jit(solution)/shard_map/while/body/eval_jaxpr/ppermute | solution.py:12
  (153 shorter events, 134.8 us)
Async XLA Ops:
  0.6 16.6 %copy-start = (f32[128,3072]{1,0:T(8,128)S(1)}, f32[128,3072]{1,0:T(8,128)}, u32[]{:S(2)}) copy-start(f32[128,3072]{1,0:T(8,128)} %param.6) | copy-start | bytes 4718596
  0.6 16.6 %copy-start.3 = (s32[1,128]{1,0:T(1,128)S(1)}, s32[1,128]{1,0:T(1,128)}, u32[]{:S(2)}) copy-start(s32[1,128]{1,0:T(1,128)} %param.7) | copy-start | bytes 1540
  72.4 23.8 %collective-permute-start = (f32[64,3072]{1,0:T(8,128)S(1)}, f32[64,3072]{1,0:T(8,128)S(1)}, u32[]{:S(2)}, u32[]{:S(2)}) collective-permute-start(f32[64,3072]{1,0:T(8,128)S(1)} %all_gather.9), channel_id=1, source_target_pairs={{0,8},{8,16},{16,24},{24,32},{32,40},{40,48},{48,56},{56,64},{64,7... | collective-permute-start | bytes 2359304 | tf_op jit(solution)/shard_map/while/body/eval_jaxpr/ppermute | solution.py:12
  149.0 23.8 %collective-permute-start = (f32[64,3072]{1,0:T(8,128)S(1)}, f32[64,3072]{1,0:T(8,128)S(1)}, u32[]{:S(2)}, u32[]{:S(2)}) collective-permute-start(f32[64,3072]{1,0:T(8,128)S(1)} %all_gather.9), channel_id=1, source_target_pairs={{0,8},{8,16},{16,24},{24,32},{32,40},{40,48},{48,56},{56,64},{64,7... | collective-permute-start | bytes 2359304 | tf_op jit(solution)/shard_map/while/body/eval_jaxpr/ppermute | solution.py:12
  225.7 23.8 %collective-permute-start = (f32[64,3072]{1,0:T(8,128)S(1)}, f32[64,3072]{1,0:T(8,128)S(1)}, u32[]{:S(2)}, u32[]{:S(2)}) collective-permute-start(f32[64,3072]{1,0:T(8,128)S(1)} %all_gather.9), channel_id=1, source_target_pairs={{0,8},{8,16},{16,24},{24,32},{32,40},{40,48},{48,56},{56,64},{64,7... | collective-permute-start | bytes 2359304 | tf_op jit(solution)/shard_map/while/body/eval_jaxpr/ppermute | solution.py:12
  302.3 23.8 %collective-permute-start = (f32[64,3072]{1,0:T(8,128)S(1)}, f32[64,3072]{1,0:T(8,128)S(1)}, u32[]{:S(2)}, u32[]{:S(2)}) collective-permute-start(f32[64,3072]{1,0:T(8,128)S(1)} %all_gather.9), channel_id=1, source_target_pairs={{0,8},{8,16},{16,24},{24,32},{32,40},{40,48},{48,56},{56,64},{64,7... | collective-permute-start | bytes 2359304 | tf_op jit(solution)/shard_map/while/body/eval_jaxpr/ppermute | solution.py:12
  378.9 23.8 %collective-permute-start = (f32[64,3072]{1,0:T(8,128)S(1)}, f32[64,3072]{1,0:T(8,128)S(1)}, u32[]{:S(2)}, u32[]{:S(2)}) collective-permute-start(f32[64,3072]{1,0:T(8,128)S(1)} %all_gather.9), channel_id=1, source_target_pairs={{0,8},{8,16},{16,24},{24,32},{32,40},{40,48},{48,56},{56,64},{64,7... | collective-permute-start | bytes 2359304 | tf_op jit(solution)/shard_map/while/body/eval_jaxpr/ppermute | solution.py:12
  455.5 23.8 %collective-permute-start = (f32[64,3072]{1,0:T(8,128)S(1)}, f32[64,3072]{1,0:T(8,128)S(1)}, u32[]{:S(2)}, u32[]{:S(2)}) collective-permute-start(f32[64,3072]{1,0:T(8,128)S(1)} %all_gather.9), channel_id=1, source_target_pairs={{0,8},{8,16},{16,24},{24,32},{32,40},{40,48},{48,56},{56,64},{64,7... | collective-permute-start | bytes 2359304 | tf_op jit(solution)/shard_map/while/body/eval_jaxpr/ppermute | solution.py:12
  532.1 23.8 %collective-permute-start = (f32[64,3072]{1,0:T(8,128)S(1)}, f32[64,3072]{1,0:T(8,128)S(1)}, u32[]{:S(2)}, u32[]{:S(2)}) collective-permute-start(f32[64,3072]{1,0:T(8,128)S(1)} %all_gather.9), channel_id=1, source_target_pairs={{0,8},{8,16},{16,24},{24,32},{32,40},{40,48},{48,56},{56,64},{64,7... | collective-permute-start | bytes 2359304 | tf_op jit(solution)/shard_map/while/body/eval_jaxpr/ppermute | solution.py:12
  608.7 23.8 %collective-permute-start = (f32[64,3072]{1,0:T(8,128)S(1)}, f32[64,3072]{1,0:T(8,128)S(1)}, u32[]{:S(2)}, u32[]{:S(2)}) collective-permute-start(f32[64,3072]{1,0:T(8,128)S(1)} %all_gather.9), channel_id=1, source_target_pairs={{0,8},{8,16},{16,24},{24,32},{32,40},{40,48},{48,56},{56,64},{64,7... | collective-permute-start | bytes 2359304 | tf_op jit(solution)/shard_map/while/body/eval_jaxpr/ppermute | solution.py:12
  685.3 23.8 %collective-permute-start = (f32[64,3072]{1,0:T(8,128)S(1)}, f32[64,3072]{1,0:T(8,128)S(1)}, u32[]{:S(2)}, u32[]{:S(2)}) collective-permute-start(f32[64,3072]{1,0:T(8,128)S(1)} %all_gather.9), channel_id=1, source_target_pairs={{0,8},{8,16},{16,24},{24,32},{32,40},{40,48},{48,56},{56,64},{64,7... | collective-permute-start | bytes 2359304 | tf_op jit(solution)/shard_map/while/body/eval_jaxpr/ppermute | solution.py:12
  762.0 23.8 %collective-permute-start = (f32[64,3072]{1,0:T(8,128)S(1)}, f32[64,3072]{1,0:T(8,128)S(1)}, u32[]{:S(2)}, u32[]{:S(2)}) collective-permute-start(f32[64,3072]{1,0:T(8,128)S(1)} %all_gather.9), channel_id=1, source_target_pairs={{0,8},{8,16},{16,24},{24,32},{32,40},{40,48},{48,56},{56,64},{64,7... | collective-permute-start | bytes 2359304 | tf_op jit(solution)/shard_map/while/body/eval_jaxpr/ppermute | solution.py:12
  838.6 23.8 %collective-permute-start = (f32[64,3072]{1,0:T(8,128)S(1)}, f32[64,3072]{1,0:T(8,128)S(1)}, u32[]{:S(2)}, u32[]{:S(2)}) collective-permute-start(f32[64,3072]{1,0:T(8,128)S(1)} %all_gather.9), channel_id=1, source_target_pairs={{0,8},{8,16},{16,24},{24,32},{32,40},{40,48},{48,56},{56,64},{64,7... | collective-permute-start | bytes 2359304 | tf_op jit(solution)/shard_map/while/body/eval_jaxpr/ppermute | solution.py:12
  915.2 23.8 %collective-permute-start = (f32[64,3072]{1,0:T(8,128)S(1)}, f32[64,3072]{1,0:T(8,128)S(1)}, u32[]{:S(2)}, u32[]{:S(2)}) collective-permute-start(f32[64,3072]{1,0:T(8,128)S(1)} %all_gather.9), channel_id=1, source_target_pairs={{0,8},{8,16},{16,24},{24,32},{32,40},{40,48},{48,56},{56,64},{64,7... | collective-permute-start | bytes 2359304 | tf_op jit(solution)/shard_map/while/body/eval_jaxpr/ppermute | solution.py:12
  991.8 23.8 %collective-permute-start = (f32[64,3072]{1,0:T(8,128)S(1)}, f32[64,3072]{1,0:T(8,128)S(1)}, u32[]{:S(2)}, u32[]{:S(2)}) collective-permute-start(f32[64,3072]{1,0:T(8,128)S(1)} %all_gather.9), channel_id=1, source_target_pairs={{0,8},{8,16},{16,24},{24,32},{32,40},{40,48},{48,56},{56,64},{64,7... | collective-permute-start | bytes 2359304 | tf_op jit(solution)/shard_map/while/body/eval_jaxpr/ppermute | solution.py:12
  1068.4 23.8 %collective-permute-start = (f32[64,3072]{1,0:T(8,128)S(1)}, f32[64,3072]{1,0:T(8,128)S(1)}, u32[]{:S(2)}, u32[]{:S(2)}) collective-permute-start(f32[64,3072]{1,0:T(8,128)S(1)} %all_gather.9), channel_id=1, source_target_pairs={{0,8},{8,16},{16,24},{24,32},{32,40},{40,48},{48,56},{56,64},{64,7... | collective-permute-start | bytes 2359304 | tf_op jit(solution)/shard_map/while/body/eval_jaxpr/ppermute | solution.py:12
  1145.0 23.8 %collective-permute-start = (f32[64,3072]{1,0:T(8,128)S(1)}, f32[64,3072]{1,0:T(8,128)S(1)}, u32[]{:S(2)}, u32[]{:S(2)}) collective-permute-start(f32[64,3072]{1,0:T(8,128)S(1)} %all_gather.9), channel_id=1, source_target_pairs={{0,8},{8,16},{16,24},{24,32},{32,40},{40,48},{48,56},{56,64},{64,7... | collective-permute-start | bytes 2359304 | tf_op jit(solution)/shard_map/while/body/eval_jaxpr/ppermute | solution.py:12
  1221.6 23.8 %collective-permute-start = (f32[64,3072]{1,0:T(8,128)S(1)}, f32[64,3072]{1,0:T(8,128)S(1)}, u32[]{:S(2)}, u32[]{:S(2)}) collective-permute-start(f32[64,3072]{1,0:T(8,128)S(1)} %all_gather.9), channel_id=1, source_target_pairs={{0,8},{8,16},{16,24},{24,32},{32,40},{40,48},{48,56},{56,64},{64,7... | collective-permute-start | bytes 2359304 | tf_op jit(solution)/shard_map/while/body/eval_jaxpr/ppermute | solution.py:12
  1298.3 23.8 %collective-permute-start = (f32[64,3072]{1,0:T(8,128)S(1)}, f32[64,3072]{1,0:T(8,128)S(1)}, u32[]{:S(2)}, u32[]{:S(2)}) collective-permute-start(f32[64,3072]{1,0:T(8,128)S(1)} %all_gather.9), channel_id=1, source_target_pairs={{0,8},{8,16},{16,24},{24,32},{32,40},{40,48},{48,56},{56,64},{64,7... | collective-permute-start | bytes 2359304 | tf_op jit(solution)/shard_map/while/body/eval_jaxpr/ppermute | solution.py:12
  1322.0 0.7 copy-start.1
  1322.0 0.7 copy-start.2
where the time goes:
time: 1320 us
  blocking collectives  631 us (48%)
  waiting for transfers between devices  370 us (28%)
  matrix products  249 us (19%)
  starting transfers between devices  33.9 us (3%)
  local copies, waits for them, and re-layouts  20.8 us (2%)
  other arithmetic  16.1 us (1%)
    psum x17, blocking collectives, finish(): weight = lax.psum(partial_weight, 'bond')  403 us
    ppermute x17, waiting for transfers between devices, from_behind(): return lax.ppermute(array, axis, pairs)  370 us
    dot_general x17, matrix products, advance(): jnp.dot(current, site_matrix, precision=lax.Precision.HIGHEST, preferred_...  249 us
    all_gather x17, blocking collectives, advance(): whole_rows = lax.all_gather(next_block, 'bond', axis=1, tiled=True)  228 us
    ppermute x17, starting transfers between devices, from_behind(): return lax.ppermute(array, axis, pairs)  33.9 us
  transfers between devices with their start and end apart: 17, of which 17 were waited for; matrix products, arithmetic and copies ran while one was open for 0% of the time, Pallas kernels for 0%

commit v1 on v0

--- a/solution.py
+++ b/solution.py
@@ -15,7 +15,7 @@
 def finish(amplitudes, chosen, block_rows, outcomes, columns, width):
     shaped = amplitudes.reshape(block_rows, outcomes, columns)
     partial_weight = jnp.sum(shaped * shaped, axis=2)
-    weight = lax.psum(partial_weight, "bond")
+    weight = jnp.sum(lax.all_gather(partial_weight, "bond"), axis=0)
     outcome_ids = jnp.arange(outcomes, dtype=jnp.int32)
     onehot = (chosen[:, None] == outcome_ids[None, :]).astype(jnp.float32)
     chosen_weight = jnp.sum(onehot * weight, axis=1)

time: 1320 us -> 1110 us (0.84)
  blocking collectives: 631 us -> 421 us
    psum x17 -> x0, blocking collectives: 403 us -> none  [finish(): weight = lax.psum(partial_weight, 'bond')]
    all_gather x0 -> x17, blocking collectives: none -> 193 us  [finish(): weight = jnp.sum(lax.all_gather(partial_weight, 'bond'), axis=0)]
where the time goes in v1:
time: 1110 us
  blocking collectives  421 us (38%)
  waiting for transfers between devices  370 us (33%)
  matrix products  249 us (22%)
  starting transfers between devices  33.9 us (3%)
  local copies, waits for them, and re-layouts  23.7 us (2%)
  other arithmetic  12.8 us (1%)
    ppermute x17, waiting for transfers between devices, from_behind(): return lax.ppermute(array, axis, pairs)  370 us
    dot_general x17, matrix products, advance(): jnp.dot(current, site_matrix, precision=lax.Precision.HIGHEST, preferred_...  249 us
    all_gather x17, blocking collectives, advance(): whole_rows = lax.all_gather(next_block, 'bond', axis=1, tiled=True)  228 us
    all_gather x17, blocking collectives, finish(): weight = jnp.sum(lax.all_gather(partial_weight, 'bond'), axis=0)  193 us
    ppermute x17, starting transfers between devices, from_behind(): return lax.ppermute(array, axis, pairs)  33.9 us
  transfers between devices with their start and end apart: 17, of which 17 were waited for; matrix products, arithmetic and copies ran while one was open for 0% of the time, Pallas kernels for 0%

profile of v1, /device:TPU:96, one launch (start us, length us, event | category | flops | bytes accessed | tf_op | source)
XLA Modules:
  0.0 1111.4 jit_solution(1509919389795837234)
XLA Ops:
  0.7 16.5 %copy.7 = f32[384,8,4,384]{3,1,2,0:T(8,128)} copy(f32[384,8,4,384]{3,2,1,0:T(4,128)} %bitcast.13) | data formatting | bytes 37748736
  17.3 1093.5 %while.18 = (s32[]{:T(128)}, f32[64,3072]{1,0:T(8,128)S(1)}, f32[128]{0:T(128)S(1)}, f32[128,384]{1,0:T(8,128)S(1)}, s32[]{:T(128)}, /*index=5*/s32[128]{0:T(128...) while((s32[]{:T(128)}, f32[64,3072]{1,0:T(8,128)S(1)}, ...), condition=%wide.region_6.7_spmd, body=%wide.region_0.6_spmd.sunk | while | flops 3624498176 | bytes 26572904 | solution.py:71
  17.5 14.6 %fusion.17 = f32[64,1536]{1,0:T(8,128)S(1)} fusion(f32[3072,1536]{1,0:T(8,128)} %get-tuple-element.314, f32[64,3072]{1,0:T(8,128)S(1)} %get-tuple-element.293, f32[128,3072]{1,0:T(8,128)S(1)} %get-tuple-element.313, s32[]{:T(128)S(6)} %select_n.103, pred[]{:T(512)} %get-tuple-element.312), kind=kOutput, calls=%fused_computation.clone.1 | convolution fusion | flops 3624075264 | bytes 20840452 | tf_op jit(solution)/shard_map/while/body/eval_jaxpr/dot_general | solution.py:52
  32.8 12.2 %all-gather.3 = f32[8,64,4]{1,2,0:T(4,128)S(1)} all-gather(f32[1,64,4]{1,2,0:T(4,128)S(1)} %copy.11), channel_id=2, replica_groups=mesh['section'=16,'bond'=8] {'bond'}, dimensions={0}, use_global_device_ids=true | all-gather | bytes 9216 | tf_op jit(solution)/shard_map/while/body/eval_jaxpr/all_gather | solution.py:18
  45.3 13.4 %all_gather.25 = f32[64,3072]{1,0:T(8,128)S(1)} all-gather(f32[64,384]{1,0:T(8,128)S(1)} %get-tuple-element.275), channel_id=1, replica_groups=mesh['section'=16,'bond'=8] {'bond'}, dimensions={1}, use_global_device_ids=true | all-gather | bytes 884736 | tf_op jit(solution)/shard_map/while/body/eval_jaxpr/all_gather | solution.py:67
  62.1 20.4 %collective-permute-done = f32[64,3072]{1,0:T(8,128)S(1)} collective-permute-done((f32[64,3072]{1,0:T(8,128)S(1)}, f32[64,3072]{1,0:T(8,128)S(1)}, u32[]{:S(2)}, u32[]{:S(2)}) %collective-permute-start) | collective-permute-done | bytes 786464 | tf_op jit(solution)/shard_map/while/body/eval_jaxpr/ppermute | solution.py:12
  82.6 14.6 %fusion.17 = f32[64,1536]{1,0:T(8,128)S(1)} fusion(f32[3072,1536]{1,0:T(8,128)} %get-tuple-element.314, f32[64,3072]{1,0:T(8,128)S(1)} %get-tuple-element.293, f32[128,3072]{1,0:T(8,128)S(1)} %get-tuple-element.313, s32[]{:T(128)S(6)} %select_n.103, pred[]{:T(512)} %get-tuple-element.312), kind=kOutput, calls=%fused_computation.clone.1 | convolution fusion | flops 3624075264 | bytes 20840452 | tf_op jit(solution)/shard_map/while/body/eval_jaxpr/dot_general | solution.py:52
  97.9 11.3 %all-gather.3 = f32[8,64,4]{1,2,0:T(4,128)S(1)} all-gather(f32[1,64,4]{1,2,0:T(4,128)S(1)} %copy.11), channel_id=2, replica_groups=mesh['section'=16,'bond'=8] {'bond'}, dimensions={0}, use_global_device_ids=true | all-gather | bytes 9216 | tf_op jit(solution)/shard_map/while/body/eval_jaxpr/all_gather | solution.py:18
  109.5 13.4 %all_gather.25 = f32[64,3072]{1,0:T(8,128)S(1)} all-gather(f32[64,384]{1,0:T(8,128)S(1)} %get-tuple-element.275), channel_id=1, replica_groups=mesh['section'=16,'bond'=8] {'bond'}, dimensions={1}, use_global_device_ids=true | all-gather | bytes 884736 | tf_op jit(solution)/shard_map/while/body/eval_jaxpr/all_gather | solution.py:67
  124.8 21.9 %collective-permute-done = f32[64,3072]{1,0:T(8,128)S(1)} collective-permute-done((f32[64,3072]{1,0:T(8,128)S(1)}, f32[64,3072]{1,0:T(8,128)S(1)}, u32[]{:S(2)}, u32[]{:S(2)}) %collective-permute-start) | collective-permute-done | bytes 786464 | tf_op jit(solution)/shard_map/while/body/eval_jaxpr/ppermute | solution.py:12
  146.9 14.6 %fusion.17 = f32[64,1536]{1,0:T(8,128)S(1)} fusion(f32[3072,1536]{1,0:T(8,128)} %get-tuple-element.314, f32[64,3072]{1,0:T(8,128)S(1)} %get-tuple-element.293, f32[128,3072]{1,0:T(8,128)S(1)} %get-tuple-element.313, s32[]{:T(128)S(6)} %select_n.103, pred[]{:T(512)} %get-tuple-element.312), kind=kOutput, calls=%fused_computation.clone.1 | convolution fusion | flops 3624075264 | bytes 20840452 | tf_op jit(solution)/shard_map/while/body/eval_jaxpr/dot_general | solution.py:52
  162.2 11.3 %all-gather.3 = f32[8,64,4]{1,2,0:T(4,128)S(1)} all-gather(f32[1,64,4]{1,2,0:T(4,128)S(1)} %copy.11), channel_id=2, replica_groups=mesh['section'=16,'bond'=8] {'bond'}, dimensions={0}, use_global_device_ids=true | all-gather | bytes 9216 | tf_op jit(solution)/shard_map/while/body/eval_jaxpr/all_gather | solution.py:18
  173.8 13.4 %all_gather.25 = f32[64,3072]{1,0:T(8,128)S(1)} all-gather(f32[64,384]{1,0:T(8,128)S(1)} %get-tuple-element.275), channel_id=1, replica_groups=mesh['section'=16,'bond'=8] {'bond'}, dimensions={1}, use_global_device_ids=true | all-gather | bytes 884736 | tf_op jit(solution)/shard_map/while/body/eval_jaxpr/all_gather | solution.py:67
  189.1 21.9 %collective-permute-done = f32[64,3072]{1,0:T(8,128)S(1)} collective-permute-done((f32[64,3072]{1,0:T(8,128)S(1)}, f32[64,3072]{1,0:T(8,128)S(1)}, u32[]{:S(2)}, u32[]{:S(2)}) %collective-permute-start) | collective-permute-done | bytes 786464 | tf_op jit(solution)/shard_map/while/body/eval_jaxpr/ppermute | solution.py:12
  211.1 14.6 %fusion.17 = f32[64,1536]{1,0:T(8,128)S(1)} fusion(f32[3072,1536]{1,0:T(8,128)} %get-tuple-element.314, f32[64,3072]{1,0:T(8,128)S(1)} %get-tuple-element.293, f32[128,3072]{1,0:T(8,128)S(1)} %get-tuple-element.313, s32[]{:T(128)S(6)} %select_n.103, pred[]{:T(512)} %get-tuple-element.312), kind=kOutput, calls=%fused_computation.clone.1 | convolution fusion | flops 3624075264 | bytes 20840452 | tf_op jit(solution)/shard_map/while/body/eval_jaxpr/dot_general | solution.py:52
  226.4 11.3 %all-gather.3 = f32[8,64,4]{1,2,0:T(4,128)S(1)} all-gather(f32[1,64,4]{1,2,0:T(4,128)S(1)} %copy.11), channel_id=2, replica_groups=mesh['section'=16,'bond'=8] {'bond'}, dimensions={0}, use_global_device_ids=true | all-gather | bytes 9216 | tf_op jit(solution)/shard_map/while/body/eval_jaxpr/all_gather | solution.py:18
  238.0 13.4 %all_gather.25 = f32[64,3072]{1,0:T(8,128)S(1)} all-gather(f32[64,384]{1,0:T(8,128)S(1)} %get-tuple-element.275), channel_id=1, replica_groups=mesh['section'=16,'bond'=8] {'bond'}, dimensions={1}, use_global_device_ids=true | all-gather | bytes 884736 | tf_op jit(solution)/shard_map/while/body/eval_jaxpr/all_gather | solution.py:67
  253.4 21.9 %collective-permute-done = f32[64,3072]{1,0:T(8,128)S(1)} collective-permute-done((f32[64,3072]{1,0:T(8,128)S(1)}, f32[64,3072]{1,0:T(8,128)S(1)}, u32[]{:S(2)}, u32[]{:S(2)}) %collective-permute-start) | collective-permute-done | bytes 786464 | tf_op jit(solution)/shard_map/while/body/eval_jaxpr/ppermute | solution.py:12
  275.4 14.6 %fusion.17 = f32[64,1536]{1,0:T(8,128)S(1)} fusion(f32[3072,1536]{1,0:T(8,128)} %get-tuple-element.314, f32[64,3072]{1,0:T(8,128)S(1)} %get-tuple-element.293, f32[128,3072]{1,0:T(8,128)S(1)} %get-tuple-element.313, s32[]{:T(128)S(6)} %select_n.103, pred[]{:T(512)} %get-tuple-element.312), kind=kOutput, calls=%fused_computation.clone.1 | convolution fusion | flops 3624075264 | bytes 20840452 | tf_op jit(solution)/shard_map/while/body/eval_jaxpr/dot_general | solution.py:52
  290.7 11.3 %all-gather.3 = f32[8,64,4]{1,2,0:T(4,128)S(1)} all-gather(f32[1,64,4]{1,2,0:T(4,128)S(1)} %copy.11), channel_id=2, replica_groups=mesh['section'=16,'bond'=8] {'bond'}, dimensions={0}, use_global_device_ids=true | all-gather | bytes 9216 | tf_op jit(solution)/shard_map/while/body/eval_jaxpr/all_gather | solution.py:18
  302.3 13.4 %all_gather.25 = f32[64,3072]{1,0:T(8,128)S(1)} all-gather(f32[64,384]{1,0:T(8,128)S(1)} %get-tuple-element.275), channel_id=1, replica_groups=mesh['section'=16,'bond'=8] {'bond'}, dimensions={1}, use_global_device_ids=true | all-gather | bytes 884736 | tf_op jit(solution)/shard_map/while/body/eval_jaxpr/all_gather | solution.py:67
  317.6 21.9 %collective-permute-done = f32[64,3072]{1,0:T(8,128)S(1)} collective-permute-done((f32[64,3072]{1,0:T(8,128)S(1)}, f32[64,3072]{1,0:T(8,128)S(1)}, u32[]{:S(2)}, u32[]{:S(2)}) %collective-permute-start) | collective-permute-done | bytes 786464 | tf_op jit(solution)/shard_map/while/body/eval_jaxpr/ppermute | solution.py:12
  339.7 14.6 %fusion.17 = f32[64,1536]{1,0:T(8,128)S(1)} fusion(f32[3072,1536]{1,0:T(8,128)} %get-tuple-element.314, f32[64,3072]{1,0:T(8,128)S(1)} %get-tuple-element.293, f32[128,3072]{1,0:T(8,128)S(1)} %get-tuple-element.313, s32[]{:T(128)S(6)} %select_n.103, pred[]{:T(512)} %get-tuple-element.312), kind=kOutput, calls=%fused_computation.clone.1 | convolution fusion | flops 3624075264 | bytes 20840452 | tf_op jit(solution)/shard_map/while/body/eval_jaxpr/dot_general | solution.py:52
  355.0 11.3 %all-gather.3 = f32[8,64,4]{1,2,0:T(4,128)S(1)} all-gather(f32[1,64,4]{1,2,0:T(4,128)S(1)} %copy.11), channel_id=2, replica_groups=mesh['section'=16,'bond'=8] {'bond'}, dimensions={0}, use_global_device_ids=true | all-gather | bytes 9216 | tf_op jit(solution)/shard_map/while/body/eval_jaxpr/all_gather | solution.py:18
  366.6 13.4 %all_gather.25 = f32[64,3072]{1,0:T(8,128)S(1)} all-gather(f32[64,384]{1,0:T(8,128)S(1)} %get-tuple-element.275), channel_id=1, replica_groups=mesh['section'=16,'bond'=8] {'bond'}, dimensions={1}, use_global_device_ids=true | all-gather | bytes 884736 | tf_op jit(solution)/shard_map/while/body/eval_jaxpr/all_gather | solution.py:67
  381.9 21.9 %collective-permute-done = f32[64,3072]{1,0:T(8,128)S(1)} collective-permute-done((f32[64,3072]{1,0:T(8,128)S(1)}, f32[64,3072]{1,0:T(8,128)S(1)}, u32[]{:S(2)}, u32[]{:S(2)}) %collective-permute-start) | collective-permute-done | bytes 786464 | tf_op jit(solution)/shard_map/while/body/eval_jaxpr/ppermute | solution.py:12
  403.9 14.6 %fusion.17 = f32[64,1536]{1,0:T(8,128)S(1)} fusion(f32[3072,1536]{1,0:T(8,128)} %get-tuple-element.314, f32[64,3072]{1,0:T(8,128)S(1)} %get-tuple-element.293, f32[128,3072]{1,0:T(8,128)S(1)} %get-tuple-element.313, s32[]{:T(128)S(6)} %select_n.103, pred[]{:T(512)} %get-tuple-element.312), kind=kOutput, calls=%fused_computation.clone.1 | convolution fusion | flops 3624075264 | bytes 20840452 | tf_op jit(solution)/shard_map/while/body/eval_jaxpr/dot_general | solution.py:52
  419.3 11.3 %all-gather.3 = f32[8,64,4]{1,2,0:T(4,128)S(1)} all-gather(f32[1,64,4]{1,2,0:T(4,128)S(1)} %copy.11), channel_id=2, replica_groups=mesh['section'=16,'bond'=8] {'bond'}, dimensions={0}, use_global_device_ids=true | all-gather | bytes 9216 | tf_op jit(solution)/shard_map/while/body/eval_jaxpr/all_gather | solution.py:18
  430.8 13.4 %all_gather.25 = f32[64,3072]{1,0:T(8,128)S(1)} all-gather(f32[64,384]{1,0:T(8,128)S(1)} %get-tuple-element.275), channel_id=1, replica_groups=mesh['section'=16,'bond'=8] {'bond'}, dimensions={1}, use_global_device_ids=true | all-gather | bytes 884736 | tf_op jit(solution)/shard_map/while/body/eval_jaxpr/all_gather | solution.py:67
  446.2 21.9 %collective-permute-done = f32[64,3072]{1,0:T(8,128)S(1)} collective-permute-done((f32[64,3072]{1,0:T(8,128)S(1)}, f32[64,3072]{1,0:T(8,128)S(1)}, u32[]{:S(2)}, u32[]{:S(2)}) %collective-permute-start) | collective-permute-done | bytes 786464 | tf_op jit(solution)/shard_map/while/body/eval_jaxpr/ppermute | solution.py:12
  468.2 14.6 %fusion.17 = f32[64,1536]{1,0:T(8,128)S(1)} fusion(f32[3072,1536]{1,0:T(8,128)} %get-tuple-element.314, f32[64,3072]{1,0:T(8,128)S(1)} %get-tuple-element.293, f32[128,3072]{1,0:T(8,128)S(1)} %get-tuple-element.313, s32[]{:T(128)S(6)} %select_n.103, pred[]{:T(512)} %get-tuple-element.312), kind=kOutput, calls=%fused_computation.clone.1 | convolution fusion | flops 3624075264 | bytes 20840452 | tf_op jit(solution)/shard_map/while/body/eval_jaxpr/dot_general | solution.py:52
  483.5 11.3 %all-gather.3 = f32[8,64,4]{1,2,0:T(4,128)S(1)} all-gather(f32[1,64,4]{1,2,0:T(4,128)S(1)} %copy.11), channel_id=2, replica_groups=mesh['section'=16,'bond'=8] {'bond'}, dimensions={0}, use_global_device_ids=true | all-gather | bytes 9216 | tf_op jit(solution)/shard_map/while/body/eval_jaxpr/all_gather | solution.py:18
  495.1 13.4 %all_gather.25 = f32[64,3072]{1,0:T(8,128)S(1)} all-gather(f32[64,384]{1,0:T(8,128)S(1)} %get-tuple-element.275), channel_id=1, replica_groups=mesh['section'=16,'bond'=8] {'bond'}, dimensions={1}, use_global_device_ids=true | all-gather | bytes 884736 | tf_op jit(solution)/shard_map/while/body/eval_jaxpr/all_gather | solution.py:67
  510.4 21.9 %collective-permute-done = f32[64,3072]{1,0:T(8,128)S(1)} collective-permute-done((f32[64,3072]{1,0:T(8,128)S(1)}, f32[64,3072]{1,0:T(8,128)S(1)}, u32[]{:S(2)}, u32[]{:S(2)}) %collective-permute-start) | collective-permute-done | bytes 786464 | tf_op jit(solution)/shard_map/while/body/eval_jaxpr/ppermute | solution.py:12
  532.5 14.6 %fusion.17 = f32[64,1536]{1,0:T(8,128)S(1)} fusion(f32[3072,1536]{1,0:T(8,128)} %get-tuple-element.314, f32[64,3072]{1,0:T(8,128)S(1)} %get-tuple-element.293, f32[128,3072]{1,0:T(8,128)S(1)} %get-tuple-element.313, s32[]{:T(128)S(6)} %select_n.103, pred[]{:T(512)} %get-tuple-element.312), kind=kOutput, calls=%fused_computation.clone.1 | convolution fusion | flops 3624075264 | bytes 20840452 | tf_op jit(solution)/shard_map/while/body/eval_jaxpr/dot_general | solution.py:52
  559.4 13.4 %all_gather.25 = f32[64,3072]{1,0:T(8,128)S(1)} all-gather(f32[64,384]{1,0:T(8,128)S(1)} %get-tuple-element.275), channel_id=1, replica_groups=mesh['section'=16,'bond'=8] {'bond'}, dimensions={1}, use_global_device_ids=true | all-gather | bytes 884736 | tf_op jit(solution)/shard_map/while/body/eval_jaxpr/all_gather | solution.py:67
  574.7 21.9 %collective-permute-done = f32[64,3072]{1,0:T(8,128)S(1)} collective-permute-done((f32[64,3072]{1,0:T(8,128)S(1)}, f32[64,3072]{1,0:T(8,128)S(1)}, u32[]{:S(2)}, u32[]{:S(2)}) %collective-permute-start) | collective-permute-done | bytes 786464 | tf_op jit(solution)/shard_map/while/body/eval_jaxpr/ppermute | solution.py:12
  596.8 14.6 %fusion.17 = f32[64,1536]{1,0:T(8,128)S(1)} fusion(f32[3072,1536]{1,0:T(8,128)} %get-tuple-element.314, f32[64,3072]{1,0:T(8,128)S(1)} %get-tuple-element.293, f32[128,3072]{1,0:T(8,128)S(1)} %get-tuple-element.313, s32[]{:T(128)S(6)} %select_n.103, pred[]{:T(512)} %get-tuple-element.312), kind=kOutput, calls=%fused_computation.clone.1 | convolution fusion | flops 3624075264 | bytes 20840452 | tf_op jit(solution)/shard_map/while/body/eval_jaxpr/dot_general | solution.py:52
  623.7 13.4 %all_gather.25 = f32[64,3072]{1,0:T(8,128)S(1)} all-gather(f32[64,384]{1,0:T(8,128)S(1)} %get-tuple-element.275), channel_id=1, replica_groups=mesh['section'=16,'bond'=8] {'bond'}, dimensions={1}, use_global_device_ids=true | all-gather | bytes 884736 | tf_op jit(solution)/shard_map/while/body/eval_jaxpr/all_gather | solution.py:67
  639.0 21.9 %collective-permute-done = f32[64,3072]{1,0:T(8,128)S(1)} collective-permute-done((f32[64,3072]{1,0:T(8,128)S(1)}, f32[64,3072]{1,0:T(8,128)S(1)}, u32[]{:S(2)}, u32[]{:S(2)}) %collective-permute-start) | collective-permute-done | bytes 786464 | tf_op jit(solution)/shard_map/while/body/eval_jaxpr/ppermute | solution.py:12
  661.0 14.6 %fusion.17 = f32[64,1536]{1,0:T(8,128)S(1)} fusion(f32[3072,1536]{1,0:T(8,128)} %get-tuple-element.314, f32[64,3072]{1,0:T(8,128)S(1)} %get-tuple-element.293, f32[128,3072]{1,0:T(8,128)S(1)} %get-tuple-element.313, s32[]{:T(128)S(6)} %select_n.103, pred[]{:T(512)} %get-tuple-element.312), kind=kOutput, calls=%fused_computation.clone.1 | convolution fusion | flops 3624075264 | bytes 20840452 | tf_op jit(solution)/shard_map/while/body/eval_jaxpr/dot_general | solution.py:52
  676.3 11.3 %all-gather.3 = f32[8,64,4]{1,2,0:T(4,128)S(1)} all-gather(f32[1,64,4]{1,2,0:T(4,128)S(1)} %copy.11), channel_id=2, replica_groups=mesh['section'=16,'bond'=8] {'bond'}, dimensions={0}, use_global_device_ids=true | all-gather | bytes 9216 | tf_op jit(solution)/shard_map/while/body/eval_jaxpr/all_gather | solution.py:18
  687.9 13.4 %all_gather.25 = f32[64,3072]{1,0:T(8,128)S(1)} all-gather(f32[64,384]{1,0:T(8,128)S(1)} %get-tuple-element.275), channel_id=1, replica_groups=mesh['section'=16,'bond'=8] {'bond'}, dimensions={1}, use_global_device_ids=true | all-gather | bytes 884736 | tf_op jit(solution)/shard_map/while/body/eval_jaxpr/all_gather | solution.py:67
  703.3 21.9 %collective-permute-done = f32[64,3072]{1,0:T(8,128)S(1)} collective-permute-done((f32[64,3072]{1,0:T(8,128)S(1)}, f32[64,3072]{1,0:T(8,128)S(1)}, u32[]{:S(2)}, u32[]{:S(2)}) %collective-permute-start) | collective-permute-done | bytes 786464 | tf_op jit(solution)/shard_map/while/body/eval_jaxpr/ppermute | solution.py:12
  725.3 14.6 %fusion.17 = f32[64,1536]{1,0:T(8,128)S(1)} fusion(f32[3072,1536]{1,0:T(8,128)} %get-tuple-element.314, f32[64,3072]{1,0:T(8,128)S(1)} %get-tuple-element.293, f32[128,3072]{1,0:T(8,128)S(1)} %get-tuple-element.313, s32[]{:T(128)S(6)} %select_n.103, pred[]{:T(512)} %get-tuple-element.312), kind=kOutput, calls=%fused_computation.clone.1 | convolution fusion | flops 3624075264 | bytes 20840452 | tf_op jit(solution)/shard_map/while/body/eval_jaxpr/dot_general | solution.py:52
  752.2 13.4 %all_gather.25 = f32[64,3072]{1,0:T(8,128)S(1)} all-gather(f32[64,384]{1,0:T(8,128)S(1)} %get-tuple-element.275), channel_id=1, replica_groups=mesh['section'=16,'bond'=8] {'bond'}, dimensions={1}, use_global_device_ids=true | all-gather | bytes 884736 | tf_op jit(solution)/shard_map/while/body/eval_jaxpr/all_gather | solution.py:67
  767.5 21.9 %collective-permute-done = f32[64,3072]{1,0:T(8,128)S(1)} collective-permute-done((f32[64,3072]{1,0:T(8,128)S(1)}, f32[64,3072]{1,0:T(8,128)S(1)}, u32[]{:S(2)}, u32[]{:S(2)}) %collective-permute-start) | collective-permute-done | bytes 786464 | tf_op jit(solution)/shard_map/while/body/eval_jaxpr/ppermute | solution.py:12
  789.6 14.6 %fusion.17 = f32[64,1536]{1,0:T(8,128)S(1)} fusion(f32[3072,1536]{1,0:T(8,128)} %get-tuple-element.314, f32[64,3072]{1,0:T(8,128)S(1)} %get-tuple-element.293, f32[128,3072]{1,0:T(8,128)S(1)} %get-tuple-element.313, s32[]{:T(128)S(6)} %select_n.103, pred[]{:T(512)} %get-tuple-element.312), kind=kOutput, calls=%fused_computation.clone.1 | convolution fusion | flops 3624075264 | bytes 20840452 | tf_op jit(solution)/shard_map/while/body/eval_jaxpr/dot_general | solution.py:52
  816.5 13.4 %all_gather.25 = f32[64,3072]{1,0:T(8,128)S(1)} all-gather(f32[64,384]{1,0:T(8,128)S(1)} %get-tuple-element.275), channel_id=1, replica_groups=mesh['section'=16,'bond'=8] {'bond'}, dimensions={1}, use_global_device_ids=true | all-gather | bytes 884736 | tf_op jit(solution)/shard_map/while/body/eval_jaxpr/all_gather | solution.py:67
  831.8 21.9 %collective-permute-done = f32[64,3072]{1,0:T(8,128)S(1)} collective-permute-done((f32[64,3072]{1,0:T(8,128)S(1)}, f32[64,3072]{1,0:T(8,128)S(1)}, u32[]{:S(2)}, u32[]{:S(2)}) %collective-permute-start) | collective-permute-done | bytes 786464 | tf_op jit(solution)/shard_map/while/body/eval_jaxpr/ppermute | solution.py:12
  853.8 14.6 %fusion.17 = f32[64,1536]{1,0:T(8,128)S(1)} fusion(f32[3072,1536]{1,0:T(8,128)} %get-tuple-element.314, f32[64,3072]{1,0:T(8,128)S(1)} %get-tuple-element.293, f32[128,3072]{1,0:T(8,128)S(1)} %get-tuple-element.313, s32[]{:T(128)S(6)} %select_n.103, pred[]{:T(512)} %get-tuple-element.312), kind=kOutput, calls=%fused_computation.clone.1 | convolution fusion | flops 3624075264 | bytes 20840452 | tf_op jit(solution)/shard_map/while/body/eval_jaxpr/dot_general | solution.py:52
  869.1 11.3 %all-gather.3 = f32[8,64,4]{1,2,0:T(4,128)S(1)} all-gather(f32[1,64,4]{1,2,0:T(4,128)S(1)} %copy.11), channel_id=2, replica_groups=mesh['section'=16,'bond'=8] {'bond'}, dimensions={0}, use_global_device_ids=true | all-gather | bytes 9216 | tf_op jit(solution)/shard_map/while/body/eval_jaxpr/all_gather | solution.py:18
  880.7 13.4 %all_gather.25 = f32[64,3072]{1,0:T(8,128)S(1)} all-gather(f32[64,384]{1,0:T(8,128)S(1)} %get-tuple-element.275), channel_id=1, replica_groups=mesh['section'=16,'bond'=8] {'bond'}, dimensions={1}, use_global_device_ids=true | all-gather | bytes 884736 | tf_op jit(solution)/shard_map/while/body/eval_jaxpr/all_gather | solution.py:67
  896.1 21.9 %collective-permute-done = f32[64,3072]{1,0:T(8,128)S(1)} collective-permute-done((f32[64,3072]{1,0:T(8,128)S(1)}, f32[64,3072]{1,0:T(8,128)S(1)}, u32[]{:S(2)}, u32[]{:S(2)}) %collective-permute-start) | collective-permute-done | bytes 786464 | tf_op jit(solution)/shard_map/while/body/eval_jaxpr/ppermute | solution.py:12
  918.1 14.6 %fusion.17 = f32[64,1536]{1,0:T(8,128)S(1)} fusion(f32[3072,1536]{1,0:T(8,128)} %get-tuple-element.314, f32[64,3072]{1,0:T(8,128)S(1)} %get-tuple-element.293, f32[128,3072]{1,0:T(8,128)S(1)} %get-tuple-element.313, s32[]{:T(128)S(6)} %select_n.103, pred[]{:T(512)} %get-tuple-element.312), kind=kOutput, calls=%fused_computation.clone.1 | convolution fusion | flops 3624075264 | bytes 20840452 | tf_op jit(solution)/shard_map/while/body/eval_jaxpr/dot_general | solution.py:52
  945.0 13.4 %all_gather.25 = f32[64,3072]{1,0:T(8,128)S(1)} all-gather(f32[64,384]{1,0:T(8,128)S(1)} %get-tuple-element.275), channel_id=1, replica_groups=mesh['section'=16,'bond'=8] {'bond'}, dimensions={1}, use_global_device_ids=true | all-gather | bytes 884736 | tf_op jit(solution)/shard_map/while/body/eval_jaxpr/all_gather | solution.py:67
  960.3 21.9 %collective-permute-done = f32[64,3072]{1,0:T(8,128)S(1)} collective-permute-done((f32[64,3072]{1,0:T(8,128)S(1)}, f32[64,3072]{1,0:T(8,128)S(1)}, u32[]{:S(2)}, u32[]{:S(2)}) %collective-permute-start) | collective-permute-done | bytes 786464 | tf_op jit(solution)/shard_map/while/body/eval_jaxpr/ppermute | solution.py:12
  982.4 14.6 %fusion.17 = f32[64,1536]{1,0:T(8,128)S(1)} fusion(f32[3072,1536]{1,0:T(8,128)} %get-tuple-element.314, f32[64,3072]{1,0:T(8,128)S(1)} %get-tuple-element.293, f32[128,3072]{1,0:T(8,128)S(1)} %get-tuple-element.313, s32[]{:T(128)S(6)} %select_n.103, pred[]{:T(512)} %get-tuple-element.312), kind=kOutput, calls=%fused_computation.clone.1 | convolution fusion | flops 3624075264 | bytes 20840452 | tf_op jit(solution)/shard_map/while/body/eval_jaxpr/dot_general | solution.py:52
  1009.3 13.4 %all_gather.25 = f32[64,3072]{1,0:T(8,128)S(1)} all-gather(f32[64,384]{1,0:T(8,128)S(1)} %get-tuple-element.275), channel_id=1, replica_groups=mesh['section'=16,'bond'=8] {'bond'}, dimensions={1}, use_global_device_ids=true | all-gather | bytes 884736 | tf_op jit(solution)/shard_map/while/body/eval_jaxpr/all_gather | solution.py:67
  1024.6 21.9 %collective-permute-done = f32[64,3072]{1,0:T(8,128)S(1)} collective-permute-done((f32[64,3072]{1,0:T(8,128)S(1)}, f32[64,3072]{1,0:T(8,128)S(1)}, u32[]{:S(2)}, u32[]{:S(2)}) %collective-permute-start) | collective-permute-done | bytes 786464 | tf_op jit(solution)/shard_map/while/body/eval_jaxpr/ppermute | solution.py:12
  1046.6 14.6 %fusion.17 = f32[64,1536]{1,0:T(8,128)S(1)} fusion(f32[3072,1536]{1,0:T(8,128)} %get-tuple-element.314, f32[64,3072]{1,0:T(8,128)S(1)} %get-tuple-element.293, f32[128,3072]{1,0:T(8,128)S(1)} %get-tuple-element.313, s32[]{:T(128)S(6)} %select_n.103, pred[]{:T(512)} %get-tuple-element.312), kind=kOutput, calls=%fused_computation.clone.1 | convolution fusion | flops 3624075264 | bytes 20840452 | tf_op jit(solution)/shard_map/while/body/eval_jaxpr/dot_general | solution.py:52
  1061.9 11.3 %all-gather.3 = f32[8,64,4]{1,2,0:T(4,128)S(1)} all-gather(f32[1,64,4]{1,2,0:T(4,128)S(1)} %copy.11), channel_id=2, replica_groups=mesh['section'=16,'bond'=8] {'bond'}, dimensions={0}, use_global_device_ids=true | all-gather | bytes 9216 | tf_op jit(solution)/shard_map/while/body/eval_jaxpr/all_gather | solution.py:18
  1073.5 13.4 %all_gather.25 = f32[64,3072]{1,0:T(8,128)S(1)} all-gather(f32[64,384]{1,0:T(8,128)S(1)} %get-tuple-element.275), channel_id=1, replica_groups=mesh['section'=16,'bond'=8] {'bond'}, dimensions={1}, use_global_device_ids=true | all-gather | bytes 884736 | tf_op jit(solution)/shard_map/while/body/eval_jaxpr/all_gather | solution.py:67
  1088.9 21.9 %collective-permute-done = f32[64,3072]{1,0:T(8,128)S(1)} collective-permute-done((f32[64,3072]{1,0:T(8,128)S(1)}, f32[64,3072]{1,0:T(8,128)S(1)}, u32[]{:S(2)}, u32[]{:S(2)}) %collective-permute-start) | collective-permute-done | bytes 786464 | tf_op jit(solution)/shard_map/while/body/eval_jaxpr/ppermute | solution.py:12
  (204 shorter events, 121.7 us)
Async XLA Ops:
  0.6 16.6 %copy-start = (f32[128,3072]{1,0:T(8,128)S(1)}, f32[128,3072]{1,0:T(8,128)}, u32[]{:S(2)}) copy-start(f32[128,3072]{1,0:T(8,128)} %param.6) | copy-start | bytes 4718596
  0.6 16.6 %copy-start.3 = (s32[1,128]{1,0:T(1,128)S(1)}, s32[1,128]{1,0:T(1,128)}, u32[]{:S(2)}) copy-start(s32[1,128]{1,0:T(1,128)} %param.7) | copy-start | bytes 1540
  58.7 23.8 %collective-permute-start = (f32[64,3072]{1,0:T(8,128)S(1)}, f32[64,3072]{1,0:T(8,128)S(1)}, u32[]{:S(2)}, u32[]{:S(2)}) collective-permute-start(f32[64,3072]{1,0:T(8,128)S(1)} %all_gather.25), channel_id=1, source_target_pairs={{0,8},{8,16},{16,24},{24,32},{32,40},{40,48},{48,56},{56,64},{64,7... | collective-permute-start | bytes 2359304 | tf_op jit(solution)/shard_map/while/body/eval_jaxpr/ppermute | solution.py:12
  122.9 23.8 %collective-permute-start = (f32[64,3072]{1,0:T(8,128)S(1)}, f32[64,3072]{1,0:T(8,128)S(1)}, u32[]{:S(2)}, u32[]{:S(2)}) collective-permute-start(f32[64,3072]{1,0:T(8,128)S(1)} %all_gather.25), channel_id=1, source_target_pairs={{0,8},{8,16},{16,24},{24,32},{32,40},{40,48},{48,56},{56,64},{64,7... | collective-permute-start | bytes 2359304 | tf_op jit(solution)/shard_map/while/body/eval_jaxpr/ppermute | solution.py:12
  187.2 23.8 %collective-permute-start = (f32[64,3072]{1,0:T(8,128)S(1)}, f32[64,3072]{1,0:T(8,128)S(1)}, u32[]{:S(2)}, u32[]{:S(2)}) collective-permute-start(f32[64,3072]{1,0:T(8,128)S(1)} %all_gather.25), channel_id=1, source_target_pairs={{0,8},{8,16},{16,24},{24,32},{32,40},{40,48},{48,56},{56,64},{64,7... | collective-permute-start | bytes 2359304 | tf_op jit(solution)/shard_map/while/body/eval_jaxpr/ppermute | solution.py:12
  251.4 23.8 %collective-permute-start = (f32[64,3072]{1,0:T(8,128)S(1)}, f32[64,3072]{1,0:T(8,128)S(1)}, u32[]{:S(2)}, u32[]{:S(2)}) collective-permute-start(f32[64,3072]{1,0:T(8,128)S(1)} %all_gather.25), channel_id=1, source_target_pairs={{0,8},{8,16},{16,24},{24,32},{32,40},{40,48},{48,56},{56,64},{64,7... | collective-permute-start | bytes 2359304 | tf_op jit(solution)/shard_map/while/body/eval_jaxpr/ppermute | solution.py:12
  315.7 23.8 %collective-permute-start = (f32[64,3072]{1,0:T(8,128)S(1)}, f32[64,3072]{1,0:T(8,128)S(1)}, u32[]{:S(2)}, u32[]{:S(2)}) collective-permute-start(f32[64,3072]{1,0:T(8,128)S(1)} %all_gather.25), channel_id=1, source_target_pairs={{0,8},{8,16},{16,24},{24,32},{32,40},{40,48},{48,56},{56,64},{64,7... | collective-permute-start | bytes 2359304 | tf_op jit(solution)/shard_map/while/body/eval_jaxpr/ppermute | solution.py:12
  380.0 23.8 %collective-permute-start = (f32[64,3072]{1,0:T(8,128)S(1)}, f32[64,3072]{1,0:T(8,128)S(1)}, u32[]{:S(2)}, u32[]{:S(2)}) collective-permute-start(f32[64,3072]{1,0:T(8,128)S(1)} %all_gather.25), channel_id=1, source_target_pairs={{0,8},{8,16},{16,24},{24,32},{32,40},{40,48},{48,56},{56,64},{64,7... | collective-permute-start | bytes 2359304 | tf_op jit(solution)/shard_map/while/body/eval_jaxpr/ppermute | solution.py:12
  444.3 23.8 %collective-permute-start = (f32[64,3072]{1,0:T(8,128)S(1)}, f32[64,3072]{1,0:T(8,128)S(1)}, u32[]{:S(2)}, u32[]{:S(2)}) collective-permute-start(f32[64,3072]{1,0:T(8,128)S(1)} %all_gather.25), channel_id=1, source_target_pairs={{0,8},{8,16},{16,24},{24,32},{32,40},{40,48},{48,56},{56,64},{64,7... | collective-permute-start | bytes 2359304 | tf_op jit(solution)/shard_map/while/body/eval_jaxpr/ppermute | solution.py:12
  508.5 23.8 %collective-permute-start = (f32[64,3072]{1,0:T(8,128)S(1)}, f32[64,3072]{1,0:T(8,128)S(1)}, u32[]{:S(2)}, u32[]{:S(2)}) collective-permute-start(f32[64,3072]{1,0:T(8,128)S(1)} %all_gather.25), channel_id=1, source_target_pairs={{0,8},{8,16},{16,24},{24,32},{32,40},{40,48},{48,56},{56,64},{64,7... | collective-permute-start | bytes 2359304 | tf_op jit(solution)/shard_map/while/body/eval_jaxpr/ppermute | solution.py:12
  572.8 23.8 %collective-permute-start = (f32[64,3072]{1,0:T(8,128)S(1)}, f32[64,3072]{1,0:T(8,128)S(1)}, u32[]{:S(2)}, u32[]{:S(2)}) collective-permute-start(f32[64,3072]{1,0:T(8,128)S(1)} %all_gather.25), channel_id=1, source_target_pairs={{0,8},{8,16},{16,24},{24,32},{32,40},{40,48},{48,56},{56,64},{64,7... | collective-permute-start | bytes 2359304 | tf_op jit(solution)/shard_map/while/body/eval_jaxpr/ppermute | solution.py:12
  637.1 23.8 %collective-permute-start = (f32[64,3072]{1,0:T(8,128)S(1)}, f32[64,3072]{1,0:T(8,128)S(1)}, u32[]{:S(2)}, u32[]{:S(2)}) collective-permute-start(f32[64,3072]{1,0:T(8,128)S(1)} %all_gather.25), channel_id=1, source_target_pairs={{0,8},{8,16},{16,24},{24,32},{32,40},{40,48},{48,56},{56,64},{64,7... | collective-permute-start | bytes 2359304 | tf_op jit(solution)/shard_map/while/body/eval_jaxpr/ppermute | solution.py:12
  701.3 23.8 %collective-permute-start = (f32[64,3072]{1,0:T(8,128)S(1)}, f32[64,3072]{1,0:T(8,128)S(1)}, u32[]{:S(2)}, u32[]{:S(2)}) collective-permute-start(f32[64,3072]{1,0:T(8,128)S(1)} %all_gather.25), channel_id=1, source_target_pairs={{0,8},{8,16},{16,24},{24,32},{32,40},{40,48},{48,56},{56,64},{64,7... | collective-permute-start | bytes 2359304 | tf_op jit(solution)/shard_map/while/body/eval_jaxpr/ppermute | solution.py:12
  765.6 23.8 %collective-permute-start = (f32[64,3072]{1,0:T(8,128)S(1)}, f32[64,3072]{1,0:T(8,128)S(1)}, u32[]{:S(2)}, u32[]{:S(2)}) collective-permute-start(f32[64,3072]{1,0:T(8,128)S(1)} %all_gather.25), channel_id=1, source_target_pairs={{0,8},{8,16},{16,24},{24,32},{32,40},{40,48},{48,56},{56,64},{64,7... | collective-permute-start | bytes 2359304 | tf_op jit(solution)/shard_map/while/body/eval_jaxpr/ppermute | solution.py:12
  829.9 23.8 %collective-permute-start = (f32[64,3072]{1,0:T(8,128)S(1)}, f32[64,3072]{1,0:T(8,128)S(1)}, u32[]{:S(2)}, u32[]{:S(2)}) collective-permute-start(f32[64,3072]{1,0:T(8,128)S(1)} %all_gather.25), channel_id=1, source_target_pairs={{0,8},{8,16},{16,24},{24,32},{32,40},{40,48},{48,56},{56,64},{64,7... | collective-permute-start | bytes 2359304 | tf_op jit(solution)/shard_map/while/body/eval_jaxpr/ppermute | solution.py:12
  894.1 23.8 %collective-permute-start = (f32[64,3072]{1,0:T(8,128)S(1)}, f32[64,3072]{1,0:T(8,128)S(1)}, u32[]{:S(2)}, u32[]{:S(2)}) collective-permute-start(f32[64,3072]{1,0:T(8,128)S(1)} %all_gather.25), channel_id=1, source_target_pairs={{0,8},{8,16},{16,24},{24,32},{32,40},{40,48},{48,56},{56,64},{64,7... | collective-permute-start | bytes 2359304 | tf_op jit(solution)/shard_map/while/body/eval_jaxpr/ppermute | solution.py:12
  958.4 23.8 %collective-permute-start = (f32[64,3072]{1,0:T(8,128)S(1)}, f32[64,3072]{1,0:T(8,128)S(1)}, u32[]{:S(2)}, u32[]{:S(2)}) collective-permute-start(f32[64,3072]{1,0:T(8,128)S(1)} %all_gather.25), channel_id=1, source_target_pairs={{0,8},{8,16},{16,24},{24,32},{32,40},{40,48},{48,56},{56,64},{64,7... | collective-permute-start | bytes 2359304 | tf_op jit(solution)/shard_map/while/body/eval_jaxpr/ppermute | solution.py:12
  1022.7 23.8 %collective-permute-start = (f32[64,3072]{1,0:T(8,128)S(1)}, f32[64,3072]{1,0:T(8,128)S(1)}, u32[]{:S(2)}, u32[]{:S(2)}) collective-permute-start(f32[64,3072]{1,0:T(8,128)S(1)} %all_gather.25), channel_id=1, source_target_pairs={{0,8},{8,16},{16,24},{24,32},{32,40},{40,48},{48,56},{56,64},{64,7... | collective-permute-start | bytes 2359304 | tf_op jit(solution)/shard_map/while/body/eval_jaxpr/ppermute | solution.py:12
  1086.9 23.8 %collective-permute-start = (f32[64,3072]{1,0:T(8,128)S(1)}, f32[64,3072]{1,0:T(8,128)S(1)}, u32[]{:S(2)}, u32[]{:S(2)}) collective-permute-start(f32[64,3072]{1,0:T(8,128)S(1)} %all_gather.25), channel_id=1, source_target_pairs={{0,8},{8,16},{16,24},{24,32},{32,40},{40,48},{48,56},{56,64},{64,7... | collective-permute-start | bytes 2359304 | tf_op jit(solution)/shard_map/while/body/eval_jaxpr/ppermute | solution.py:12
  1110.7 0.7 copy-start.1
  1110.7 0.7 copy-start.2
